TPU v7x, 32 devices: a whole 2x2x4 slice. The times are simulated.
32 devices in a mesh: rows: 4 (over z), chan: 8 (over y, x, core).
Axes of the slice: x: 2, y: 2, z: 4, core: 2. Of those that a mesh axis runs over, the one named last changes fastest.
Arguments:
- feats: bfloat16 [64, 1024, 1024], P('rows', 'chan'), may hold values from -140 to 140
- norm_gain: float32 [1024], P('chan'), may hold values from 0.1 to 1.9
- proj_weight: float32 [8, 1024], P(None, 'chan'), may hold values from -320 to 320
- chan_bias: float32 [1024], P('chan'), may hold values from -8 to -2
Outputs:
- mixed: bfloat16 [64, 1024, 1024], P('rows', 'chan')
All inputs are finite; a program needn't handle non-finite values.
Results may differ from a plain program's by a relative error of at most 0.001.
Values sent between devices are 32-bit elements; how exact they have to be, the bound alone decides.
A program may use at most 128 MiB of HBM per device.

v0:
```python
import jax
import jax.numpy as jnp
from jax import lax
from jax.sharding import PartitionSpec as P

CHANNELS = 1024
EPSILON = 1e-05


def advance(current, row_weights, row_rate):
    edge_zero = jnp.zeros_like(current[:, :1])
    left_side = jnp.concatenate([edge_zero, current[:, :-1]], axis=1)
    right_side = jnp.concatenate([current[:, 1:], edge_zero], axis=1)
    blended = (
        row_weights[0][None, :] * left_side
        + row_weights[1][None, :] * current
        + row_weights[2][None, :] * right_side
    )
    return (1.0 - row_rate) * blended


def coefficients(logits, chan_bias, offset):
    weights = jax.nn.softmax(logits[:, offset : offset + 3, :], axis=1)
    rates = jax.nn.sigmoid(logits[:, 6 + offset // 3, :][:, None, :] + chan_bias[None, :, None])
    return (weights, rates)


def sweep_rows(start, weights, rates, drive, reverse, keep):

    def sweep_row_step(current, inputs):
        row_weights, row_rate, row_drive = inputs
        current = advance(current, row_weights, row_rate) + row_drive
        return (current, current if keep else None)

    return lax.scan(sweep_row_step, start, (weights, rates, drive), reverse=reverse)


def carry_through(start, weights, rates, reverse):

    def carry_row_step(current, inputs):
        return (advance(current, inputs[0], inputs[1]), None)

    finished, _ = lax.scan(carry_row_step, start, (weights, rates), reverse=reverse)
    return finished


def shards(feats, norm_gain, proj_weight, chan_bias):
    logit_scale = CHANNELS ** (-0.5)
    values = feats.astype(jnp.float32)
    squares = jnp.sum(values * values, axis=1)
    square_total = lax.psum(squares, "chan")
    inverse = 1.0 / jnp.sqrt(square_total / CHANNELS + EPSILON)
    normed = values * inverse[:, None, :] * norm_gain[None, :, None]
    projected = jnp.einsum(
        "jc,rcw->rjw",
        proj_weight,
        normed,
        precision=lax.Precision.HIGHEST,
        preferred_element_type=jnp.float32,
    )
    logits = lax.psum(projected, "chan") * logit_scale
    down_weights, down_rate = coefficients(logits, chan_bias, 0)
    up_weights, up_rate = coefficients(logits, chan_bias, 3)
    down_drive = jnp.sqrt(down_rate) * normed
    up_drive = jnp.sqrt(up_rate) * normed
    anchor = jnp.zeros((feats.shape[1], feats.shape[2]), jnp.float32)
    down_local, _ = sweep_rows(anchor, down_weights, down_rate, down_drive, False, False)
    up_local, _ = sweep_rows(anchor, up_weights, up_rate, up_drive, True, False)
    gathered, down_ends, up_ends = (
        lax.all_gather(logits, "rows", axis=0, tiled=True),
        lax.all_gather(down_local, "rows", axis=0, tiled=True),
        lax.all_gather(up_local, "rows", axis=0, tiled=True),
    )
    position = lax.axis_index("rows")
    devices = lax.axis_size("rows")
    block_rows = logits.shape[0]
    local_chans = feats.shape[1]

    def down_visit(visited, current):
        visited = jnp.asarray(visited).astype(jnp.int32)
        block_logits = lax.dynamic_slice_in_dim(gathered, visited * block_rows, block_rows, 0)
        block_weights, block_rates = coefficients(block_logits, chan_bias, 0)
        block_end = lax.dynamic_slice_in_dim(down_ends, visited * local_chans, local_chans, 0)
        return carry_through(current, block_weights, block_rates, False) + block_end

    def up_visit(turn, current):
        visited = (devices - 1 - jnp.asarray(turn)).astype(jnp.int32)
        block_logits = lax.dynamic_slice_in_dim(gathered, visited * block_rows, block_rows, 0)
        block_weights, block_rates = coefficients(block_logits, chan_bias, 3)
        block_end = lax.dynamic_slice_in_dim(up_ends, visited * local_chans, local_chans, 0)
        return carry_through(current, block_weights, block_rates, True) + block_end

    down_in = lax.fori_loop(0, position, down_visit, anchor)
    up_in = lax.fori_loop(0, devices - 1 - position, up_visit, anchor)
    _, down_rows = sweep_rows(down_in, down_weights, down_rate, down_drive, False, True)
    _, up_rows = sweep_rows(up_in, up_weights, up_rate, up_drive, True, True)
    return (down_rows * up_rows).astype(jnp.bfloat16)


def solution(mesh):
    in_specs = (P("rows", "chan", None), P("chan"), P(None, "chan"), P("chan"))
    out_specs = P("rows", "chan", None)
    return jax.shard_map(shards, mesh=mesh, in_specs=in_specs, out_specs=out_specs, check_vma=False)
```

profile of v0, /device:TPU:0, one launch (start us, length us, event | category | flops | bytes accessed | tf_op | source)
XLA Modules:
  0.0 489.4 jit_solution(14477030094933963573)
XLA Ops:
  6.5 3.9 fusion.28
  10.5 56.0 %all-reduce.15.cloned.1.call-done = f32[16,1024]{1,0:T(8,128)} async-done(((f32[16,1024]{1,0:T(8,128)}), f32[16,1024]{1,0:T(8,128)}) %all-reduce.15.cloned.1.call-update) | async-done | bytes 65552 | tf_op jit(solution)/shard_map/psum | solution.py:51
  67.4 7.7 %fusion.36 = f32[16,8,1024]{2,1,0:T(8,128)} fusion(bf16[16,128,1024]{2,1,0:T(8,128)(2,1)} %param.20, f32[128]{0:T(128)} %param.21, f32[16,1024]{1,0:T(8,128)S(1)} %add_rsqrt_fusion, f32[8,128]{1,0:T(8,128)S(1)} %copy-done), kind=kOutput, calls=%fused_computation.76 | convolution fusion | flops 207618048 | bytes 4788736 | tf_op jit(solution)/shard_map/jc,rcw->rjw/dot_general | solution.py:54
  75.1 54.3 %all-reduce.17.cloned.1.call-done = f32[16,8,1024]{2,1,0:T(8,128)} async-done(((f32[16,8,1024]{2,1,0:T(8,128)}), f32[16,8,1024]{2,1,0:T(8,128)}) %all-reduce.17.cloned.1.call-update) | async-done | bytes 524304 | tf_op jit(solution)/shard_map/psum | solution.py:61
  131.1 15.1 %fusion.30 = (f32[16,128,1024]{2,1,0:T(8,128)}, f32[16,128,1024]{2,1,0:T(8,128)}, f32[16,128,1024]{2,1,0:T(8,128)}, f32[16,128,1024]{2,1,0:T(8,128)}) fusion(bf16[16,128,1024]{2,1,0:T(8,128)(2,1)} %param.20, f32[128]{0:T(128)S(1)} %copy-done.6, f32[16,1024]{1,0:T(8,128)S(1)} %add_rsqrt_fusion, f32[128]{0:T(128)S(1)} %copy-done.5, ...), kind=kLoop, calls=%fused_computation.68 | loop fusion | flops 27262976 | bytes 37946368 | tf_op jit(solution)/shard_map/mul | solution.py:65
  146.2 30.4 %while.121 = (s32[]{:T(128)}, f32[128,1024]{1,0:T(8,128)S(1)}, f32[16,128,1024]{2,1,0:T(8,128)}, f32[16,3,1024]{2,1,0:T(4,128)S(1)}, f32[16,128,1024]{2,1,0:T(8,...) while((s32[]{:T(128)}, f32[128,1024]{1,0:T(8,128)S(1)}, ...), condition=%wide.region_18.19_spmd.clone, body=%wide.region_17.18_spmd.clone.sunk | while | flops 1310726 | bytes 6325412 | solution.py:35
  178.1 31.0 %while.120 = (s32[]{:T(128)}, f32[128,1024]{1,0:T(8,128)S(1)}, f32[16,128,1024]{2,1,0:T(8,128)}, f32[16,3,1024]{2,1,0:T(4,128)S(1)}, f32[16,128,1024]{2,1,0:T(8,128)}, /*index=5*/s32[]{:T(128)}, s32[]{:T(128)}, s32[]{}, s32[]{}) while((s32[]{:T(128)}, f32[128,1024]{1,0:T(8,128)S(1)}, f32[16,128,1024]{2,1,0:T(8,128)}, ...), condition=%wide.region_6.0_spmd.clone, body=%wide.region_5.0_spmd.clone.sunk | while | flops 1310725 | bytes 6325392 | solution.py:35
  178.4 1.6 bitcast_add_fusion.8
  180.3 1.6 bitcast_add_fusion.8
  182.3 1.7 bitcast_add_fusion.8
  184.2 1.7 bitcast_add_fusion.8
  190.1 1.6 bitcast_add_fusion.8
  192.0 1.6 bitcast_add_fusion.8
  195.8 1.6 bitcast_add_fusion.8
  197.8 1.6 bitcast_add_fusion.8
  201.7 1.6 bitcast_add_fusion.8
  203.6 1.6 bitcast_add_fusion.8
  207.5 1.6 bitcast_add_fusion.8
  209.9 12.7 %all-gather.8.cloned.1.call-done = f32[512,1024]{1,0:T(8,128)} async-done(((f32[128,1024]{1,0:T(8,128)}), f32[512,1024]{1,0:T(8,128)}) %all-gather.8.cloned.1.call-update) | async-done | bytes 2097168 | tf_op jit(solution)/shard_map/all_gather | solution.py:72
  222.6 45.9 %all-gather.4.cloned.1.call-done = f32[64,8,1024]{2,1,0:T(8,128)} async-done(((f32[16,8,1024]{2,1,0:T(8,128)}), f32[64,8,1024]{2,1,0:T(8,128)}) %all-gather.4.cloned.1.call-update) | async-done | bytes 2097168 | tf_op jit(solution)/shard_map/all_gather | solution.py:70
  268.6 112.8 %while.118 = (s32[]{:T(128)}, f32[128,1024]{1,0:T(8,128)S(1)}, s32[]{:T(128)}, f32[64,8,1024]{2,1,0:T(8,128)}, f32[128]{0:T(128)S(1)}, /*index=5*/f32[512,1024]{...) while((s32[]{:T(128)}, f32[128,1024]{1,0:T(8,128)S(1)}, ...), condition=%wide.region_24.25_spmd, body=%wide.region_19.24_spmd.sunk | while | flops 9568278 | bytes 15501354 | solution.py:94
  269.9 5.4 %add_divide_fusion.7 = f32[16,128,1024]{2,1,0:T(8,128)} fusion(f32[128]{0:T(128)S(1)} %get-tuple-element.1319, f32[16,1024]{1,0:T(8,128)S(1)} %bitcast.131), kind=kLoop, calls=%fused_computation.30.clone.1 | loop fusion | flops 8388608 | bytes 8454656 | tf_op jit(solution)/shard_map/while/body/div | solution.py:24
  276.8 28.4 %while.123 = (s32[]{:T(128)}, f32[128,1024]{1,0:T(8,128)S(1)}, f32[16,128,1024]{2,1,0:T(8,128)}, f32[16,3,1024]{2,1,0:T(4,128)S(1)}, s32[]{:T(128)}, /*index=5*/s32[]{:T(128)}, s32[]{:T(128)}, s32[]{}, s32[]{}) while((s32[]{:T(128)}, f32[128,1024]{1,0:T(8,128)S(1)}, f32[16,128,1024]{2,1,0:T(8,128)}, f32[16,3,1024]{2,1,0:T(4,128)S(1)}, ...), condition=%wide.region_23.23_spmd, body=%wide.region_22.22_spmd.sunk | while | flops 917509 | bytes 4752529 | solution.py:43
  307.5 5.4 %add_divide_fusion.7 = f32[16,128,1024]{2,1,0:T(8,128)} fusion(f32[128]{0:T(128)S(1)} %get-tuple-element.1319, f32[16,1024]{1,0:T(8,128)S(1)} %bitcast.131), kind=kLoop, calls=%fused_computation.30.clone.1 | loop fusion | flops 8388608 | bytes 8454656 | tf_op jit(solution)/shard_map/while/body/div | solution.py:24
  314.4 28.3 %while.123 = (s32[]{:T(128)}, f32[128,1024]{1,0:T(8,128)S(1)}, f32[16,128,1024]{2,1,0:T(8,128)}, f32[16,3,1024]{2,1,0:T(4,128)S(1)}, s32[]{:T(128)}, /*index=5*/s32[]{:T(128)}, s32[]{:T(128)}, s32[]{}, s32[]{}) while((s32[]{:T(128)}, f32[128,1024]{1,0:T(8,128)S(1)}, f32[16,128,1024]{2,1,0:T(8,128)}, f32[16,3,1024]{2,1,0:T(4,128)S(1)}, ...), condition=%wide.region_23.23_spmd, body=%wide.region_22.22_spmd.sunk | while | flops 917509 | bytes 4752529 | solution.py:43
  345.0 5.4 %add_divide_fusion.7 = f32[16,128,1024]{2,1,0:T(8,128)} fusion(f32[128]{0:T(128)S(1)} %get-tuple-element.1319, f32[16,1024]{1,0:T(8,128)S(1)} %bitcast.131), kind=kLoop, calls=%fused_computation.30.clone.1 | loop fusion | flops 8388608 | bytes 8454656 | tf_op jit(solution)/shard_map/while/body/div | solution.py:24
  351.9 28.3 %while.123 = (s32[]{:T(128)}, f32[128,1024]{1,0:T(8,128)S(1)}, f32[16,128,1024]{2,1,0:T(8,128)}, f32[16,3,1024]{2,1,0:T(4,128)S(1)}, s32[]{:T(128)}, /*index=5*/s32[]{:T(128)}, s32[]{:T(128)}, s32[]{}, s32[]{}) while((s32[]{:T(128)}, f32[128,1024]{1,0:T(8,128)S(1)}, f32[16,128,1024]{2,1,0:T(8,128)}, f32[16,3,1024]{2,1,0:T(4,128)S(1)}, ...), condition=%wide.region_23.23_spmd, body=%wide.region_22.22_spmd.sunk | while | flops 917509 | bytes 4752529 | solution.py:43
  381.4 4.3 broadcast.113.clone.1
  385.6 41.8 %while.119 = (s32[]{:T(128)}, f32[128,1024]{1,0:T(8,128)S(1)}, f32[16,128,1024]{2,1,0:T(8,128)}, f32[16,128,1024]{2,1,0:T(8,128)}, f32[16,3,1024]{2,1,0:T(4,128)...) while((s32[]{:T(128)}, f32[128,1024]{1,0:T(8,128)S(1)}, ...), condition=%wide.region_26.27_spmd, body=%wide.region_25.26_spmd.sunk | while | flops 1048581 | bytes 5801121 | solution.py:35
  385.9 2.4 bitcast_dynamic-update-slice_fusion.5
  388.5 2.4 bitcast_dynamic-update-slice_fusion.5
  391.1 2.4 bitcast_dynamic-update-slice_fusion.5
  393.7 2.4 bitcast_dynamic-update-slice_fusion.5
  396.3 2.4 bitcast_dynamic-update-slice_fusion.5
  398.9 2.4 bitcast_dynamic-update-slice_fusion.5
  401.5 2.4 bitcast_dynamic-update-slice_fusion.5
  404.2 2.4 bitcast_dynamic-update-slice_fusion.5
  406.8 2.4 bitcast_dynamic-update-slice_fusion.5
  409.4 2.4 bitcast_dynamic-update-slice_fusion.5
  412.0 2.4 bitcast_dynamic-update-slice_fusion.5
  414.6 2.4 bitcast_dynamic-update-slice_fusion.5
  417.2 2.4 bitcast_dynamic-update-slice_fusion.5
  419.8 2.4 bitcast_dynamic-update-slice_fusion.5
  422.4 2.4 bitcast_dynamic-update-slice_fusion.5
  425.1 2.4 bitcast_dynamic-update-slice_fusion.5
  427.5 4.3 broadcast.113.clone
  431.8 41.8 %while.116 = (s32[]{:T(128)}, f32[128,1024]{1,0:T(8,128)S(1)}, f32[16,128,1024]{2,1,0:T(8,128)}, f32[16,128,1024]{2,1,0:T(8,128)}, f32[16,3,1024]{2,1,0:T(4,128)...) while((s32[]{:T(128)}, f32[128,1024]{1,0:T(8,128)S(1)}, ...), condition=%wide.region_14.15_spmd, body=%wide.region_13.14_spmd.sunk | while | flops 1048580 | bytes 5801609 | solution.py:35
  432.0 2.4 bitcast_dynamic-update-slice_fusion.4
  434.6 2.4 bitcast_dynamic-update-slice_fusion.4
  437.2 2.4 bitcast_dynamic-update-slice_fusion.4
  439.9 2.4 bitcast_dynamic-update-slice_fusion.4
  442.5 2.4 bitcast_dynamic-update-slice_fusion.4
  445.1 2.4 bitcast_dynamic-update-slice_fusion.4
  447.7 2.4 bitcast_dynamic-update-slice_fusion.4
  450.3 2.4 bitcast_dynamic-update-slice_fusion.4
  452.9 2.4 bitcast_dynamic-update-slice_fusion.4
  455.5 2.4 bitcast_dynamic-update-slice_fusion.4
  458.1 2.4 bitcast_dynamic-update-slice_fusion.4
  460.8 2.4 bitcast_dynamic-update-slice_fusion.4
  463.4 2.4 bitcast_dynamic-update-slice_fusion.4
  466.0 2.4 bitcast_dynamic-update-slice_fusion.4
  468.6 2.4 bitcast_dynamic-update-slice_fusion.4
  471.2 2.4 bitcast_dynamic-update-slice_fusion.4
  473.6 9.3 %multiply_convert_fusion = bf16[16,128,1024]{2,1,0:T(8,128)(2,1)} fusion(f32[16,128,1024]{2,1,0:T(8,128)} %get-tuple-element.568, f32[16,128,1024]{2,1,0:T(8,128)} %get-tuple-element.571), kind=kLoop, calls=%fused_computation.71 | loop fusion | flops 4194304 | bytes 20971520 | tf_op jit(solution)/shard_map/convert_element_type | solution.py:97
  (373 shorter events, 148.7 us)
Async XLA Ops:
  6.5 60.8 %copy-start = (f32[8,128]{1,0:T(8,128)S(1)}, f32[8,128]{1,0:T(8,128)}, u32[]{:S(2)}) copy-start(f32[8,128]{1,0:T(8,128)} %param.22) | copy-start | bytes 12292
  6.5 124.5 %copy-start.6 = (f32[128]{0:T(128)S(1)}, f32[128]{0:T(128)}, u32[]{:S(2)}) copy-start(f32[128]{0:T(128)} %param.21) | copy-start | bytes 1540
  6.5 124.6 %copy-start.5 = (f32[128]{0:T(128)S(1)}, f32[128]{0:T(128)}, u32[]{:S(2)}) copy-start(f32[128]{0:T(128)} %param.23) | copy-start | bytes 1540
  6.5 60.0 %all-reduce.15.cloned.1.call-start = ((), (), s32[]{:S(2)}) async-start(), calls=%async_computation | async-start | bytes 131072 | tf_op jit(solution)/shard_map/psum | solution.py:51
  10.5 119.0 %all-reduce.17.cloned.1.call-start = ((), (), s32[]{:S(2)}) async-start(), calls=%async_computation.1 | async-start | bytes 1048576 | tf_op jit(solution)/shard_map/psum | solution.py:61
  75.1 147.5 %all-gather.8.cloned.1.call-start = ((), (), s32[]{:S(2)}) async-start(), calls=%async_computation.4 | async-start | bytes 2621440 | tf_op jit(solution)/shard_map/all_gather | solution.py:72
  130.5 47.0 %copy-start.4 = (f32[16,8,1024]{2,1,0:T(8,128)}, f32[16,8,1024]{2,1,0:T(8,128)S(1)}, u32[]{:S(2)}) copy-start(f32[16,8,1024]{2,1,0:T(8,128)S(1)} %broadcast_multiply_fusion) | copy-start | bytes 1572868
  176.7 0.8 copy-start.2
  177.5 91.0 %all-gather.4.cloned.1.call-start = ((), (), s32[]{:S(2)}) async-start(), calls=%async_computation.2 | async-start | bytes 2621440 | tf_op jit(solution)/shard_map/all_gather | solution.py:70
  178.1 249.4 %all-gather.6.cloned.1.call-start = ((), (), s32[]{:S(2)}) async-start(), calls=%async_computation.3 | async-start | bytes 2621440 | tf_op jit(solution)/shard_map/all_gather | solution.py:71
  209.1 0.8 copy-start.3
  473.6 9.3 %copy-start.1 = (f32[8,128]{1,0:T(8,128)S(1)}, f32[8,128]{1,0:T(8,128)}, u32[]{:S(2)}) copy-start(f32[8,128]{1,0:T(8,128)} %param.22) | copy-start | bytes 12292
Sparse Core Ops, SparseCore 0:
  10.6 55.8 all-reduce.14
  75.2 54.1 all-reduce.16
  177.6 44.9 all-gather.7
  224.0 44.4 all-gather.3
  269.9 44.4 all-gather.5
where the time goes:
time: 494 us; the launch traced here: 489 us
  other arithmetic  258 us (52%)
  waiting for transfers between devices  169 us (34%)
  local copies, waits for them, and re-layouts  38.3 us (8%)
  between operations  13.3 us (3%)
  matrix products  7.69 us (2%)
    dynamic_update_slice x32, other arithmetic, sweep_rows(): lax.scan(sweep_row_step, start, (weights, rates, drive), reverse=reverse)  76.6 us
    mul x48, other arithmetic, advance(): return (1.0 - row_rate) * blended  73.1 us
    psum x1, waiting for transfers between devices, shards(): square_total = lax.psum(squares, 'chan')  56 us
    psum x1, waiting for transfers between devices, shards(): logits = lax.psum(projected, 'chan') * logit_scale  54.3 us
    add x32, other arithmetic, sweep_row_step(): current = advance(current, row_weights, row_rate) + row_drive  51.8 us
    all_gather x1, waiting for transfers between devices, shards(): lax.all_gather(logits, 'rows', axis=0, tiled=True)  45.9 us
    slice x112, local copies, waits for them, and re-layouts, advance(): left_side = jnp.concatenate([edge_zero, current[:, :-1]], axis=1)  22.6 us
    div x3, other arithmetic, coefficients(): jax.nn.sigmoid(logits[:, 6 + offset // 3, :][:, None, :] + chan_bias[None...  16.3 us
  transfers between devices with their start and end apart: 5, of which 4 were waited for; matrix products, arithmetic and copies ran while one was open for 38% of the time, Pallas kernels for 0%

commit v1 on v0

--- a/solution.py
+++ b/solution.py
@@ -48,7 +48,11 @@
     logit_scale = CHANNELS ** (-0.5)
     values = feats.astype(jnp.float32)
     squares = jnp.sum(values * values, axis=1)
-    square_total = lax.psum(squares, "chan")
+    square_total = squares
+    for hop in (1, 2, 4):
+        square_total = square_total + lax.ppermute(
+            square_total, "chan", [(dev, dev ^ hop) for dev in range(8)]
+        )
     inverse = 1.0 / jnp.sqrt(square_total / CHANNELS + EPSILON)
     normed = values * inverse[:, None, :] * norm_gain[None, :, None]
     projected = jnp.einsum(

time: 494 us -> 450 us (0.911)
  waiting for transfers between devices: 169 us -> 121 us
  starting transfers between devices: 0.17 us -> 5.52 us
    psum x1 -> x0, waiting for transfers between devices: 56 us -> none  [shards(): square_total = lax.psum(squares, 'chan')]
    ppermute x0 -> x3, waiting for transfers between devices: none -> 5.7 us  [shards(): lax.ppermute(square_total, 'chan', [(dev, dev ^ hop) for dev in range(8)])]
    ppermute x0 -> x3, starting transfers between devices: none -> 5.39 us  [shards(): lax.ppermute(square_total, 'chan', [(dev, dev ^ hop) for dev in range(8)])]
  transfers between devices with their start and end apart: 5 -> 7, of which waited for: 4 -> 6; matrix products, arithmetic and copies ran while one was open for 38% -> 42% of each run, Pallas kernels for 0% -> 0%
where the time goes in v1:
time: 450 us; the launch traced here: 446 us
  other arithmetic  256 us (57%)
  waiting for transfers between devices  121 us (27%)
  local copies, waits for them, and re-layouts  38.3 us (9%)
  between operations  13.3 us (3%)
  matrix products  7.69 us (2%)
  starting transfers between devices  5.52 us (1%)
    dynamic_update_slice x32, other arithmetic, sweep_rows(): lax.scan(sweep_row_step, start, (weights, rates, drive), reverse=reverse)  76.6 us
    mul x48, other arithmetic, advance(): return (1.0 - row_rate) * blended  73.1 us
    psum x1, waiting for transfers between devices, shards(): logits = lax.psum(projected, 'chan') * logit_scale  56.5 us
    add x32, other arithmetic, sweep_row_step(): current = advance(current, row_weights, row_rate) + row_drive  51.8 us
    all_gather x1, waiting for transfers between devices, shards(): lax.all_gather(logits, 'rows', axis=0, tiled=True)  46.1 us
    slice x112, local copies, waits for them, and re-layouts, advance(): left_side = jnp.concatenate([edge_zero, current[:, :-1]], axis=1)  22.6 us
    div x3, other arithmetic, coefficients(): jax.nn.sigmoid(logits[:, 6 + offset // 3, :][:, None, :] + chan_bias[None...  16.4 us
    mul x1, other arithmetic, shards(): up_drive = jnp.sqrt(up_rate) * normed  15.2 us
  transfers between devices with their start and end apart: 7, of which 6 were waited for; matrix products, arithmetic and copies ran while one was open for 42% of the time, Pallas kernels for 0%

profile of v1, /device:TPU:0, one launch (start us, length us, event | category | flops | bytes accessed | tf_op | source)
XLA Modules:
  0.0 445.5 jit_solution(16679190661572288843)
XLA Ops:
  6.5 3.3 fusion.28
  11.3 2.9 collective-permute-start.1
  14.2 2.4 collective-permute-done.1
  16.6 1.9 collective-permute-start.2
  18.6 2.4 collective-permute-done.2
  21.0 7.7 %fusion.36 = f32[16,8,1024]{2,1,0:T(8,128)} fusion(bf16[16,128,1024]{2,1,0:T(8,128)(2,1)} %param.20, f32[128]{0:T(128)} %param.21, f32[16,1024]{1,0:T(8,128)S(1)} %add_rsqrt_fusion, f32[8,128]{1,0:T(8,128)S(1)} %copy-done), kind=kOutput, calls=%fused_computation.76 | convolution fusion | flops 207618048 | bytes 4788736 | tf_op jit(solution)/shard_map/jc,rcw->rjw/dot_general | solution.py:58
  28.7 56.5 %all-reduce.14.cloned.1.call-done = f32[16,8,1024]{2,1,0:T(8,128)} async-done(((f32[16,8,1024]{2,1,0:T(8,128)}), f32[16,8,1024]{2,1,0:T(8,128)}) %all-reduce.14.cloned.1.call-update) | async-done | bytes 524304 | tf_op jit(solution)/shard_map/psum | solution.py:65
  86.9 15.2 %fusion.30 = (f32[16,128,1024]{2,1,0:T(8,128)}, f32[16,128,1024]{2,1,0:T(8,128)}, f32[16,128,1024]{2,1,0:T(8,128)}, f32[16,128,1024]{2,1,0:T(8,128)}) fusion(bf16[16,128,1024]{2,1,0:T(8,128)(2,1)} %param.20, f32[128]{0:T(128)S(1)} %copy-done.6, f32[16,1024]{1,0:T(8,128)S(1)} %add_rsqrt_fusion, f32[128]{0:T(128)S(1)} %copy-done.5, ...), kind=kLoop, calls=%fused_computation.68 | loop fusion | flops 27262976 | bytes 37946368 | tf_op jit(solution)/shard_map/mul | solution.py:69
  102.1 30.4 %while.121 = (s32[]{:T(128)}, f32[128,1024]{1,0:T(8,128)S(1)}, f32[16,128,1024]{2,1,0:T(8,128)}, f32[16,3,1024]{2,1,0:T(4,128)S(1)}, f32[16,128,1024]{2,1,0:T(8,...) while((s32[]{:T(128)}, f32[128,1024]{1,0:T(8,128)S(1)}, ...), condition=%wide.region_17.18_spmd.clone, body=%wide.region_16.17_spmd.clone.sunk | while | flops 1310726 | bytes 6325412 | solution.py:35
  134.1 31.0 %while.120 = (s32[]{:T(128)}, f32[128,1024]{1,0:T(8,128)S(1)}, f32[16,128,1024]{2,1,0:T(8,128)}, f32[16,3,1024]{2,1,0:T(4,128)S(1)}, f32[16,128,1024]{2,1,0:T(8,128)}, /*index=5*/s32[]{:T(128)}, s32[]{:T(128)}, s32[]{}, s32[]{}) while((s32[]{:T(128)}, f32[128,1024]{1,0:T(8,128)S(1)}, f32[16,128,1024]{2,1,0:T(8,128)}, ...), condition=%wide.region_5.0_spmd.clone, body=%wide.region_4.0_spmd.clone.sunk | while | flops 1310725 | bytes 6325392 | solution.py:35
  138.3 1.7 bitcast_add_fusion.8
  140.2 1.6 bitcast_add_fusion.8
  146.0 1.6 bitcast_add_fusion.8
  148.0 1.6 bitcast_add_fusion.8
  151.8 1.6 bitcast_add_fusion.8
  153.8 1.6 bitcast_add_fusion.8
  157.6 1.6 bitcast_add_fusion.8
  159.6 1.6 bitcast_add_fusion.8
  165.9 12.5 %all-gather.8.cloned.1.call-done = f32[512,1024]{1,0:T(8,128)} async-done(((f32[128,1024]{1,0:T(8,128)}), f32[512,1024]{1,0:T(8,128)}) %all-gather.8.cloned.1.call-update) | async-done | bytes 2097168 | tf_op jit(solution)/shard_map/all_gather | solution.py:76
  178.4 46.1 %all-gather.4.cloned.1.call-done = f32[64,8,1024]{2,1,0:T(8,128)} async-done(((f32[16,8,1024]{2,1,0:T(8,128)}), f32[64,8,1024]{2,1,0:T(8,128)}) %all-gather.4.cloned.1.call-update) | async-done | bytes 2097168 | tf_op jit(solution)/shard_map/all_gather | solution.py:74
  224.6 112.8 %while.118 = (s32[]{:T(128)}, f32[128,1024]{1,0:T(8,128)S(1)}, s32[]{:T(128)}, f32[64,8,1024]{2,1,0:T(8,128)}, f32[128]{0:T(128)S(1)}, /*index=5*/f32[512,1024]{...) while((s32[]{:T(128)}, f32[128,1024]{1,0:T(8,128)S(1)}, ...), condition=%wide.region_23.24_spmd, body=%wide.region_18.23_spmd.sunk | while | flops 9568278 | bytes 15501354 | solution.py:98
  225.9 5.5 %add_divide_fusion.7 = f32[16,128,1024]{2,1,0:T(8,128)} fusion(f32[128]{0:T(128)S(1)} %get-tuple-element.1319, f32[16,1024]{1,0:T(8,128)S(1)} %bitcast.131), kind=kLoop, calls=%fused_computation.30.clone.1 | loop fusion | flops 8388608 | bytes 8454656 | tf_op jit(solution)/shard_map/while/body/div | solution.py:24
  232.8 28.4 %while.123 = (s32[]{:T(128)}, f32[128,1024]{1,0:T(8,128)S(1)}, f32[16,128,1024]{2,1,0:T(8,128)}, f32[16,3,1024]{2,1,0:T(4,128)S(1)}, s32[]{:T(128)}, /*index=5*/s32[]{:T(128)}, s32[]{:T(128)}, s32[]{}, s32[]{}) while((s32[]{:T(128)}, f32[128,1024]{1,0:T(8,128)S(1)}, f32[16,128,1024]{2,1,0:T(8,128)}, f32[16,3,1024]{2,1,0:T(4,128)S(1)}, ...), condition=%wide.region_22.22_spmd, body=%wide.region_21.21_spmd.sunk | while | flops 917509 | bytes 4752529 | solution.py:43
  263.5 5.5 %add_divide_fusion.7 = f32[16,128,1024]{2,1,0:T(8,128)} fusion(f32[128]{0:T(128)S(1)} %get-tuple-element.1319, f32[16,1024]{1,0:T(8,128)S(1)} %bitcast.131), kind=kLoop, calls=%fused_computation.30.clone.1 | loop fusion | flops 8388608 | bytes 8454656 | tf_op jit(solution)/shard_map/while/body/div | solution.py:24
  270.4 28.3 %while.123 = (s32[]{:T(128)}, f32[128,1024]{1,0:T(8,128)S(1)}, f32[16,128,1024]{2,1,0:T(8,128)}, f32[16,3,1024]{2,1,0:T(4,128)S(1)}, s32[]{:T(128)}, /*index=5*/s32[]{:T(128)}, s32[]{:T(128)}, s32[]{}, s32[]{}) while((s32[]{:T(128)}, f32[128,1024]{1,0:T(8,128)S(1)}, f32[16,128,1024]{2,1,0:T(8,128)}, f32[16,3,1024]{2,1,0:T(4,128)S(1)}, ...), condition=%wide.region_22.22_spmd, body=%wide.region_21.21_spmd.sunk | while | flops 917509 | bytes 4752529 | solution.py:43
  301.0 5.5 %add_divide_fusion.7 = f32[16,128,1024]{2,1,0:T(8,128)} fusion(f32[128]{0:T(128)S(1)} %get-tuple-element.1319, f32[16,1024]{1,0:T(8,128)S(1)} %bitcast.131), kind=kLoop, calls=%fused_computation.30.clone.1 | loop fusion | flops 8388608 | bytes 8454656 | tf_op jit(solution)/shard_map/while/body/div | solution.py:24
  307.9 28.3 %while.123 = (s32[]{:T(128)}, f32[128,1024]{1,0:T(8,128)S(1)}, f32[16,128,1024]{2,1,0:T(8,128)}, f32[16,3,1024]{2,1,0:T(4,128)S(1)}, s32[]{:T(128)}, /*index=5*/s32[]{:T(128)}, s32[]{:T(128)}, s32[]{}, s32[]{}) while((s32[]{:T(128)}, f32[128,1024]{1,0:T(8,128)S(1)}, f32[16,128,1024]{2,1,0:T(8,128)}, f32[16,3,1024]{2,1,0:T(4,128)S(1)}, ...), condition=%wide.region_22.22_spmd, body=%wide.region_21.21_spmd.sunk | while | flops 917509 | bytes 4752529 | solution.py:43
  337.4 4.3 broadcast.113.clone.1
  341.7 41.8 %while.119 = (s32[]{:T(128)}, f32[128,1024]{1,0:T(8,128)S(1)}, f32[16,128,1024]{2,1,0:T(8,128)}, f32[16,128,1024]{2,1,0:T(8,128)}, f32[16,3,1024]{2,1,0:T(4,128)...) while((s32[]{:T(128)}, f32[128,1024]{1,0:T(8,128)S(1)}, ...), condition=%wide.region_25.26_spmd, body=%wide.region_24.25_spmd.sunk | while | flops 1048581 | bytes 5801121 | solution.py:35
  341.9 2.4 bitcast_dynamic-update-slice_fusion.5
  344.5 2.4 bitcast_dynamic-update-slice_fusion.5
  347.1 2.4 bitcast_dynamic-update-slice_fusion.5
  349.7 2.4 bitcast_dynamic-update-slice_fusion.5
  352.4 2.4 bitcast_dynamic-update-slice_fusion.5
  355.0 2.4 bitcast_dynamic-update-slice_fusion.5
  357.6 2.4 bitcast_dynamic-update-slice_fusion.5
  360.2 2.4 bitcast_dynamic-update-slice_fusion.5
  362.8 2.4 bitcast_dynamic-update-slice_fusion.5
  365.4 2.4 bitcast_dynamic-update-slice_fusion.5
  368.1 2.4 bitcast_dynamic-update-slice_fusion.5
  370.7 2.4 bitcast_dynamic-update-slice_fusion.5
  373.3 2.4 bitcast_dynamic-update-slice_fusion.5
  375.9 2.4 bitcast_dynamic-update-slice_fusion.5
  378.5 2.4 bitcast_dynamic-update-slice_fusion.5
  381.1 2.4 bitcast_dynamic-update-slice_fusion.5
  383.6 4.3 broadcast.113.clone
  387.9 41.8 %while.116 = (s32[]{:T(128)}, f32[128,1024]{1,0:T(8,128)S(1)}, f32[16,128,1024]{2,1,0:T(8,128)}, f32[16,128,1024]{2,1,0:T(8,128)}, f32[16,3,1024]{2,1,0:T(4,128)...) while((s32[]{:T(128)}, f32[128,1024]{1,0:T(8,128)S(1)}, ...), condition=%wide.region_13.14_spmd, body=%wide.region_12.13_spmd.sunk | while | flops 1048580 | bytes 5801609 | solution.py:35
  388.1 2.4 bitcast_dynamic-update-slice_fusion.4
  390.7 2.4 bitcast_dynamic-update-slice_fusion.4
  393.3 2.4 bitcast_dynamic-update-slice_fusion.4
  395.9 2.4 bitcast_dynamic-update-slice_fusion.4
  398.5 2.4 bitcast_dynamic-update-slice_fusion.4
  401.2 2.4 bitcast_dynamic-update-slice_fusion.4
  403.8 2.4 bitcast_dynamic-update-slice_fusion.4
  406.4 2.4 bitcast_dynamic-update-slice_fusion.4
  409.0 2.4 bitcast_dynamic-update-slice_fusion.4
  411.6 2.4 bitcast_dynamic-update-slice_fusion.4
  414.2 2.4 bitcast_dynamic-update-slice_fusion.4
  416.8 2.4 bitcast_dynamic-update-slice_fusion.4
  419.4 2.4 bitcast_dynamic-update-slice_fusion.4
  422.1 2.4 bitcast_dynamic-update-slice_fusion.4
  424.6 2.4 bitcast_dynamic-update-slice_fusion.4
  427.2 2.4 bitcast_dynamic-update-slice_fusion.4
  429.7 9.3 %multiply_convert_fusion = bf16[16,128,1024]{2,1,0:T(8,128)(2,1)} fusion(f32[16,128,1024]{2,1,0:T(8,128)} %get-tuple-element.568, f32[16,128,1024]{2,1,0:T(8,128)} %get-tuple-element.571), kind=kLoop, calls=%fused_computation.71 | loop fusion | flops 4194304 | bytes 20971520 | tf_op jit(solution)/shard_map/convert_element_type | solution.py:101
  (378 shorter events, 154.3 us)
Async XLA Ops:
  6.5 14.4 %copy-start = (f32[8,128]{1,0:T(8,128)S(1)}, f32[8,128]{1,0:T(8,128)}, u32[]{:S(2)}) copy-start(f32[8,128]{1,0:T(8,128)} %param.22) | copy-start | bytes 12292
  6.5 80.4 %copy-start.6 = (f32[128]{0:T(128)S(1)}, f32[128]{0:T(128)}, u32[]{:S(2)}) copy-start(f32[128]{0:T(128)} %param.21) | copy-start | bytes 1540
  6.5 80.4 %copy-start.5 = (f32[128]{0:T(128)S(1)}, f32[128]{0:T(128)}, u32[]{:S(2)}) copy-start(f32[128]{0:T(128)} %param.23) | copy-start | bytes 1540
  6.5 78.7 %all-reduce.14.cloned.1.call-start = ((), (), s32[]{:S(2)}) async-start(), calls=%async_computation | async-start | bytes 1048576 | tf_op jit(solution)/shard_map/psum | solution.py:65
  9.8 1.5 collective-permute-start
  11.3 5.3 %collective-permute-start.1 = (f32[16,1024]{1,0:T(8,128)S(1)}, f32[16,1024]{1,0:T(8,128)S(1)}, u32[]{:S(2)}, u32[]{:S(2)}) collective-permute-start(f32[16,1024]{1,0:T(8,128)S(1)} %add.341), channel_id=1, source_target_pairs={{0,2},{1,3},{2,0},{3,1},{4,6},{5,7},{6,4},{7,5},{8,10},{9,11},{10,... | collective-permute-start | bytes 196616 | tf_op jit(solution)/shard_map/ppermute | solution.py:53
  16.6 4.3 collective-permute-start.2
  28.7 149.8 %all-gather.8.cloned.1.call-start = ((), (), s32[]{:S(2)}) async-start(), calls=%async_computation.3 | async-start | bytes 2621440 | tf_op jit(solution)/shard_map/all_gather | solution.py:76
  86.3 47.1 %copy-start.4 = (f32[16,8,1024]{2,1,0:T(8,128)}, f32[16,8,1024]{2,1,0:T(8,128)S(1)}, u32[]{:S(2)}) copy-start(f32[16,8,1024]{2,1,0:T(8,128)S(1)} %broadcast_multiply_fusion) | copy-start | bytes 1572868
  132.5 0.8 copy-start.2
  133.3 91.2 %all-gather.4.cloned.1.call-start = ((), (), s32[]{:S(2)}) async-start(), calls=%async_computation.1 | async-start | bytes 2621440 | tf_op jit(solution)/shard_map/all_gather | solution.py:74
  134.1 249.4 %all-gather.6.cloned.1.call-start = ((), (), s32[]{:S(2)}) async-start(), calls=%async_computation.2 | async-start | bytes 2621440 | tf_op jit(solution)/shard_map/all_gather | solution.py:75
  165.1 0.8 copy-start.3
  429.7 9.3 %copy-start.1 = (f32[8,128]{1,0:T(8,128)S(1)}, f32[8,128]{1,0:T(8,128)}, u32[]{:S(2)}) copy-start(f32[8,128]{1,0:T(8,128)} %param.22) | copy-start | bytes 12292
Sparse Core Ops, SparseCore 0:
  28.8 56.4 all-reduce.13
  133.4 44.9 all-gather.7
  180.0 44.4 all-gather.3
  225.9 44.4 all-gather.5
